TPU v7x, 512 devices: a whole 4x8x8 slice. The times are simulated.
512 devices in a mesh: row: 16 (over x_hi, z), col: 32 (over y, x_lo, core).
Axes of the slice: x: 4 (x_hi: 2, x_lo: 2; x = x_hi * 2 + x_lo), y: 8, z: 8, core: 2. Of those that a mesh axis runs over, the one named last changes fastest.
Arguments:
- activations: bfloat16 [1024, 28672], P('row', 'col'), may hold values from -0.1875 to 0.1875
- cotangent: bfloat16 [1024, 16384], P('col', 'row'), may hold values from -6 to 6
- down_weight: bfloat16 [28672, 16384], P('col', 'row'), may hold values from -0.046875 to 0.046875
- row_order: int32 [1024], replicated, may hold values from 0 to 1023, each once
Outputs:
- weight_grad: bfloat16 [28672, 16384], P('col', 'row')
- input_grad: bfloat16 [1024, 28672], P('row', 'col')
Inputs may be any that keep to these rules, and one draw needn't show every extreme that they name: `row_order`: each of the 1024 rows is named exactly once.
All inputs are finite; a program needn't handle non-finite values.
Results may differ from a plain program's by a relative error of at most 0.001.
Values may be sent and summed in bfloat16 or wider, within the bound.
A program may use at most 64 MiB of HBM per device.

v0:
```python
import jax
import jax.numpy as jnp
from jax import lax
from jax.sharding import PartitionSpec as P


def contract_rows(left, right):
    return lax.dot_general(
        left, right, (((0,), (0,)), ((), ())), preferred_element_type=jnp.float32
    )


def contract_cols(left, right):
    return lax.dot_general(
        left, right, (((1,), (1,)), ((), ())), preferred_element_type=jnp.float32
    )


def body(activations, cotangent, down_weight, row_order):
    gathered = lax.all_gather(cotangent, "col", axis=0, tiled=True)
    aligned = jnp.take(gathered, row_order, axis=0)
    all_rows = lax.all_gather(activations, "row", axis=0, tiled=True)
    weight_total = contract_rows(all_rows, aligned)
    weight_grad = weight_total.astype(jnp.bfloat16)
    partial_sums = contract_cols(aligned, down_weight)
    summed = lax.psum_scatter(partial_sums, "row", scatter_dimension=0, tiled=True)
    input_grad = summed.astype(jnp.bfloat16)
    return (weight_grad, input_grad)


def solution(mesh):
    in_specs = (P("row", "col"), P("col", "row"), P("col", "row"), P())
    out_specs = (P("col", "row"), P("row", "col"))
    return jax.shard_map(body, mesh=mesh, in_specs=in_specs, out_specs=out_specs, check_vma=False)
```

profile of v0, /device:TPU:1, one launch (start us, length us, event | category | flops | bytes accessed | tf_op | source)
XLA Modules:
  0.0 398.9 jit_solution(9003948174916197972)
XLA Ops:
  7.2 0.0 copy-start
  7.2 0.0 all-gather.3.cloned.1.call-start
  7.2 0.7 all-gather.3.cloned.1.call-update
  7.9 0.0 all-gather.5.cloned.1.call-start
  8.0 0.7 all-gather.5.cloned.1.call-update
  8.7 0.0 reduce-scatter.2.cloned.1.call-start
  8.7 0.7 compare_and_fusion
  9.4 0.7 fusion.1
  10.1 73.1 %all-gather.3.cloned.1.call-done = bf16[1024,1024]{1,0:T(8,128)(2,1)} async-done(((bf16[32,1024]{1,0:T(8,128)(2,1)}), bf16[1024,1024]{1,0:T(8,128)(2,1)}) %all-gather.3.cloned.1.call-update) | async-done | bytes 2097168 | tf_op jit(solution)/shard_map/all_gather | solution.py:20
  83.2 7.9 %gather_fusion = bf16[1024,1024]{1,0:T(8,128)(2,1)} fusion(bf16[1024,1024]{1,0:T(8,128)(2,1)} %all-gather.3.cloned.1.call-done, s32[1024]{0:T(1024)S(1)} %fusion.1), kind=kCustom, calls=%fused_computation | custom fusion | bytes 4198400 | tf_op jit(solution)/shard_map/jit(_take)/gather | solution.py:21
  91.1 0.0 copy-done
  91.1 5.8 %fusion = f32[1024,896]{1,0:T(8,128)} fusion(bf16[896,1024]{1,0:T(8,128)(2,1)S(1)} %copy-done, bf16[1024,1024]{1,0:T(8,128)(2,1)} %gather_fusion, pred[1024]{0:T(1024)(128)(4,1)S(1)} %compare_and_fusion), kind=kOutput, calls=%fused_computation.3 | convolution fusion | flops 1880096768 | bytes 7603200 | tf_op jit(solution)/shard_map/dot_general | solution.py:14
  96.8 0.0 reduce-scatter.2.cloned.1.call-update
  96.9 75.5 %all-gather.5.cloned.1.call-done = bf16[1024,896]{1,0:T(8,128)(2,1)} async-done(((bf16[64,896]{1,0:T(8,128)(2,1)}), bf16[1024,896]{1,0:T(8,128)(2,1)}) %all-gather.5.cloned.1.call-update) | async-done | bytes 1835024 | tf_op jit(solution)/shard_map/all_gather | solution.py:22
  172.4 5.9 %convert_bitcast_fusion = bf16[896,1024]{0,1:T(8,128)(2,1)} fusion(bf16[1024,896]{1,0:T(8,128)(2,1)} %all-gather.5.cloned.1.call-done, bf16[1024,1024]{1,0:T(8,128)(2,1)} %gather_fusion, pred[1024]{0:T(1024)(128)(4,1)S(1)} %compare_and_fusion), kind=kOutput, calls=%fused_computation.2 | convolution fusion | flops 1881014272 | bytes 5768192 | tf_op jit(solution)/shard_map/dot_general | solution.py:8
  178.3 3.8 copy.6
  182.1 208.7 %reduce-scatter.2.cloned.1.call-done = f32[64,896]{1,0:T(8,128)} async-done(((f32[1024,896]{1,0:T(8,128)}), f32[64,896]{1,0:T(8,128)}) %reduce-scatter.2.cloned.1.call-update) | async-done | bytes 229392 | tf_op jit(solution)/shard_map/reduce_scatter | solution.py:26
  390.7 1.6 convert_element_type.11
Async XLA Ops:
  7.2 83.9 %copy-start = (bf16[896,1024]{1,0:T(8,128)(2,1)S(1)}, bf16[896,1024]{1,0:T(8,128)(2,1)}, u32[]{:S(2)}) copy-start(bf16[896,1024]{1,0:T(8,128)(2,1)} %param.6) | copy-start | bytes 5505028
  7.2 76.0 %all-gather.3.cloned.1.call-start = ((), (), s32[]{:S(2)}) async-start(), calls=%async_computation.1 | async-start | bytes 2162688 | tf_op jit(solution)/shard_map/all_gather | solution.py:20
  7.9 164.5 %all-gather.5.cloned.1.call-start = ((), (), s32[]{:S(2)}) async-start(), calls=%async_computation.2 | async-start | bytes 1949696 | tf_op jit(solution)/shard_map/all_gather | solution.py:22
  8.7 382.1 %reduce-scatter.2.cloned.1.call-start = ((), (), s32[]{:S(2)}) async-start(), calls=%async_computation.3 | async-start | bytes 3899392 | tf_op jit(solution)/shard_map/reduce_scatter | solution.py:26
Sparse Core Ops, SparseCore 0:
  10.2 72.9 all-gather.2
  86.4 85.9 all-gather.4
  177.0 213.7 reduce-scatter.1
where the time goes:
time: 402 us; the launch traced here: 399 us
  waiting for transfers between devices  359 us (89%)
  between operations  13.8 us (3%)
  local copies, waits for them, and re-layouts  11.7 us (3%)
  matrix products  11.7 us (3%)
    reduce_scatter x1, waiting for transfers between devices, body(): lax.psum_scatter(partial_sums, 'row', scatter_dimension=0, tiled=True)  209 us
    all_gather x1, waiting for transfers between devices, body(): all_rows = lax.all_gather(activations, 'row', axis=0, tiled=True)  75.5 us
    all_gather x1, waiting for transfers between devices, body(): gathered = lax.all_gather(cotangent, 'col', axis=0, tiled=True)  73.1 us
  transfers between devices with their start and end apart: 3, of which 3 were waited for; matrix products, arithmetic and copies ran while one was open for 6% of the time, Pallas kernels for 0%

commit v1 on v0

v1 whole, which is shorter than its diff:
```python
import functools

import jax
import jax.numpy as jnp
from jax import lax
from jax.experimental import pallas as pl
from jax.experimental.pallas import tpu as pltpu
from jax.sharding import PartitionSpec as P

MESH = pl.DeviceIdType.MESH
RING = 8
FAR = RING // 2
GROUPS = [(FAR, 0), (FAR, 1)]
for _d in (3, 2, 1):
    GROUPS += [(_d, 0), (_d, 1), (-_d, 0), (-_d, 1)]
GROUPS += [(0, 0), (0, 1)]
PLACE = {g: i for i, g in enumerate(GROUPS)}
F32 = jnp.float32
BF16 = jnp.bfloat16


def z_place(distance, half):
    if distance in (FAR, -FAR):
        distance = FAR
    return PLACE[(distance, half)]


def hops(direction, stream):
    return FAR if (direction == 1) == (stream == 0) else FAR - 1


STREAMS = [(d, s) for s in (0, 1) for d in (1, -1)]


def dot_nt(a, b):
    return lax.dot_general(a, b, (((1,), (1,)), ((), ())), preferred_element_type=F32)


def dot_tn(a, b):
    return lax.dot_general(a, b, (((0,), (0,)), ((), ())), preferred_element_type=F32)


def kernel(
    act, cot, weight, order, wgrad, igrad,
    cot_all, act_all, w_vmem, place_col, pick, aligned, partial,
    out_val, out_scale, in_val, in_scale,
    g_send, g_recv, s_send, s_recv, a_send, a_recv, r_send, r_recv, c_send, c_recv, local_sem,
):
    row, col = lax.axis_index("row"), lax.axis_index("col")
    xh, z = row // RING, lax.rem(row, RING)
    y, xl, core = col // 4, lax.rem(col, 4) // 2, lax.rem(col, 2)

    def at_z(step):
        return (xh * RING + lax.rem(z + step + RING, RING), col)

    def at_y(step):
        return (row, lax.rem(y + step + RING, RING) * 4 + xl * 2 + core)

    x_far = ((1 - xh) * RING + z, col)
    x_near = (row, y * 4 + (1 - xl) * 2 + core)
    sibling = (row, y * 4 + xl * 2 + 1 - core)

    rows_g = cot.shape[0]
    rows_a, hidden = act.shape
    total = cot_all.shape[0]
    half = total // 2

    def g_slot(core_d, y_d, x_d):
        return cot_all.at[pl.ds(core_d * half + ((y_d % RING) * 2 + x_d) * rows_g, rows_g)]

    def a_rows(distance, h):
        return pl.ds(z_place(distance, h) * rows_a, rows_a)

    def remote(src, dst, send, recv, device):
        return pltpu.make_async_remote_copy(
            src_ref=src, dst_ref=dst, send_sem=send, recv_sem=recv, device_id=device, device_id_type=MESH
        )

    barrier = pltpu.get_barrier_semaphore()
    partners = (at_y(1), at_y(-1), x_near, sibling, at_z(1), at_z(-1), x_far)
    for device in partners:
        pl.semaphore_signal(barrier, inc=1, device_id=device, device_id_type=MESH)
    pl.semaphore_wait(barrier, len(partners))

    sent = []

    def start(copy):
        copy.start()
        sent.append(copy)
        return copy

    g_ring = {}
    n = 0
    for step in range(1, FAR + 1):
        for d, s in STREAMS:
            if step <= hops(d, s):
                src = cot if (step == 1 and s == 0) else g_slot(0, -d * (step - 1), s)
                g_ring[(step, d, s)] = remote(src, g_slot(0, -d * step, s), g_send.at[n], g_recv.at[n], at_y(d))
                n += 1
    g_near = remote(cot, g_slot(0, 0, 1), g_send.at[n], g_recv.at[n], x_near)
    s_copies = {}
    for y_d in range(RING):
        for x_d in range(2):
            i = y_d * 2 + x_d
            src = cot if i == 0 else g_slot(0, y_d, x_d)
            s_copies[(y_d, x_d)] = remote(src, g_slot(1, y_d, x_d), s_send.at[i], s_recv.at[i], sibling)

    a_ring = {}
    n = 0
    for step in range(1, FAR + 1):
        for d, s in STREAMS:
            if step <= hops(d, s):
                src = act if (step == 1 and s == 0) else act_all.at[a_rows(-d * (step - 1), s)]
                a_ring[(step, d, s)] = remote(src, act_all.at[a_rows(-d * step, s)], a_send.at[n], a_recv.at[n], at_z(d))
                n += 1
    a_far = remote(act, act_all.at[a_rows(0, 1)], a_send.at[n], a_recv.at[n], x_far)

    start(g_near)
    start(g_ring[(1, 1, 0)])
    start(g_ring[(1, -1, 0)])
    start(a_far)
    start(a_ring[(1, 1, 0)])
    start(a_ring[(1, -1, 0)])
    start(s_copies[(0, 0)])
    own_g = pltpu.make_async_copy(cot, g_slot(0, 0, 0), local_sem.at[0])
    own_a = pltpu.make_async_copy(act, act_all.at[a_rows(0, 0)], local_sem.at[1])
    own_w = pltpu.make_async_copy(weight, w_vmem, local_sem.at[2])
    own_g.start()
    own_a.start()
    own_w.start()

    r = order[...]
    spot = (
        lax.rem(r // 32 + core, 2) * half
        + lax.rem(r // 128 - y + RING, RING) * (2 * rows_g)
        + lax.rem(r // 64 + xl, 2) * rows_g
        + lax.rem(r, 32)
    ).astype(F32)
    for b in range(total // 128):
        place_col[b * 128:(b + 1) * 128, :] = jnp.transpose(jnp.broadcast_to(spot[b:b + 1, :], (128, 128)))

    g_near.wait_recv()
    start(g_ring[(1, 1, 1)])
    start(g_ring[(1, -1, 1)])
    start(s_copies[(0, 1)])
    a_far.wait_recv()
    start(a_ring[(1, 1, 1)])
    start(a_ring[(1, -1, 1)])

    lanes = lax.broadcasted_iota(jnp.int32, (rows_a, 128), 1).astype(F32)

    def build_pick(first, last):
        for i in range(first, last):
            distance, h = GROUPS[i]
            shard = lax.rem(xh + h, 2) * RING + lax.rem(z + distance + RING, RING)
            want = place_col[pl.ds(pl.multiple_of(shard * rows_a, rows_a), rows_a), :]
            for j in range(total // 128):
                hit = jnp.where(want == lanes + float(j * 128), 1.0, 0.0).astype(F32)
                pick[i * rows_a:(i + 1) * rows_a, j * 128:(j + 1) * 128] = hit.astype(BF16)

    def g_step(step):
        for d, s in STREAMS:
            if step <= hops(d, s):
                g_ring[(step, d, s)].wait_recv()
                if step < hops(d, s):
                    start(g_ring[(step + 1, d, s)])
                start(s_copies[((-d * step) % RING, s)])

    def a_step(step):
        for d, s in STREAMS:
            if step <= hops(d, s):
                a_ring[(step, d, s)].wait_recv()
                if step < hops(d, s):
                    start(a_ring[(step + 1, d, s)])

    build_pick(0, 6)
    g_step(1)
    build_pick(6, 11)
    g_step(2)
    a_step(1)
    build_pick(11, 16)
    g_step(3)
    a_step(2)
    g_step(4)
    own_g.wait()
    for key in s_copies:
        s_copies[key].wait_recv()
    own_w.wait()

    def sums(first, last):
        rows = slice(first * rows_a, last * rows_a)
        aligned[rows, :] = jnp.dot(pick[rows, :], cot_all[...], preferred_element_type=F32).astype(BF16)
        partial[rows, :] = dot_nt(aligned[rows, :], w_vmem[...])

    def part_of(distance, h):
        i = z_place(distance, h)
        return partial[i * rows_a:(i + 1) * rows_a, :]

    def encode(value, slot):
        top = jnp.maximum(jnp.max(jnp.abs(value), axis=0, keepdims=True), 1e-34)
        out_val[slot] = jnp.round(value * (32767.0 / top)).astype(jnp.int32).astype(jnp.int16)
        out_scale[slot] = top * (1.0 / 32767.0)

    def decode(slot):
        return in_val[slot].astype(jnp.int32).astype(F32) * in_scale[slot]

    r_copies = {}
    n = 0
    for level in range(FAR, 0, -1):
        for d, h in STREAMS:
            if level <= hops(d, h):
                r_copies[(level, d, h)] = (
                    n,
                    remote(out_val.at[n], in_val.at[n], r_send.at[n], r_recv.at[n], at_z(d)),
                    remote(out_scale.at[n], in_scale.at[n], c_send.at[n], c_recv.at[n], at_z(d)),
                )
                n += 1
    x_copies = (
        n,
        remote(out_val.at[n], in_val.at[n], r_send.at[n], r_recv.at[n], x_far),
        remote(out_scale.at[n], in_scale.at[n], c_send.at[n], c_recv.at[n], x_far),
    )

    def post(entry, value):
        slot, data, scale = entry
        encode(value, slot)
        start(data)
        start(scale)

    def fetch(entry):
        slot, data, scale = entry
        data.wait_recv()
        scale.wait_recv()
        return decode(slot)

    def first_send(level, d, h):
        post(r_copies[(level, d, h)], part_of(level * d, h))

    def next_send(level, d, h):
        post(r_copies[(level, d, h)], fetch(r_copies[(level + 1, d, h)]) + part_of(level * d, h))

    def wgrad_tiles(first, last):
        def tile(t, carry):
            at = pl.ds(pl.multiple_of(t * 128, 128), 128)
            wgrad[at, :] = dot_tn(act_all[:, at], aligned[...]).astype(BF16)
            return carry

        lax.fori_loop(first, last, tile, 0)

    sums(0, 2)
    first_send(4, 1, 0)
    first_send(4, -1, 1)
    a_step(3)
    sums(2, 6)
    first_send(3, 1, 1)
    first_send(3, -1, 0)
    next_send(3, 1, 0)
    next_send(3, -1, 1)
    a_step(4)
    own_a.wait()
    sums(6, 10)
    for level in (2, 1):
        next_send(level, 1, 1)
        next_send(level, -1, 0)
        next_send(level, 1, 0)
        next_send(level, -1, 1)
        if level == 2:
            sums(10, 14)
            sums(14, 16)
            wgrad_tiles(0, 2)
        else:
            wgrad_tiles(2, 4)
    away = part_of(0, 1) + fetch(r_copies[(1, 1, 1)])
    away = away + fetch(r_copies[(1, -1, 1)])
    post(x_copies, away)
    home = part_of(0, 0) + fetch(r_copies[(1, -1, 0)])
    home = home + fetch(r_copies[(1, 1, 0)])
    wgrad_tiles(4, 7)
    igrad[...] = (home + fetch(x_copies)).astype(BF16)
    for copy in sent:
        copy.wait_send()


def body(activations, cotangent, down_weight, row_order):
    rows_a, hidden = activations.shape
    rows_g, width = cotangent.shape
    total = row_order.shape[0]
    any_space = pl.BlockSpec(memory_space=pl.ANY)
    vmem = pl.BlockSpec(memory_space=pltpu.VMEM)
    slots = 15
    dma = pltpu.SemaphoreType.DMA
    return pl.pallas_call(
        kernel,
        out_shape=(
            jax.ShapeDtypeStruct((hidden, width), BF16),
            jax.ShapeDtypeStruct((rows_a, hidden), BF16),
        ),
        in_specs=[any_space, any_space, any_space, vmem],
        out_specs=(vmem, vmem),
        scratch_shapes=[
            pltpu.VMEM((total, width), BF16),
            pltpu.VMEM((total, hidden), BF16),
            pltpu.VMEM((hidden, width), BF16),
            pltpu.VMEM((total, 128), F32),
            pltpu.VMEM((total, total), BF16),
            pltpu.VMEM((total, width), BF16),
            pltpu.VMEM((total, hidden), F32),
            pltpu.VMEM((slots, rows_a, hidden), jnp.int16),
            pltpu.VMEM((slots, 1, hidden), F32),
            pltpu.VMEM((slots, rows_a, hidden), jnp.int16),
            pltpu.VMEM((slots, 1, hidden), F32),
            dma((15,)), dma((15,)), dma((16,)), dma((16,)), dma((15,)), dma((15,)),
            dma((15,)), dma((15,)), dma((15,)), dma((15,)), dma((3,)),
        ],
        compiler_params=pltpu.CompilerParams(
            collective_id=0, has_side_effects=True, vmem_limit_bytes=48 * 1024 * 1024
        ),
    )(activations, cotangent, down_weight, row_order.reshape(total // 128, 128))


def solution(mesh):
    in_specs = (P("row", "col"), P("col", "row"), P("col", "row"), P())
    out_specs = (P("col", "row"), P("row", "col"))
    return jax.shard_map(body, mesh=mesh, in_specs=in_specs, out_specs=out_specs, check_vma=False)
```

time: 402 us -> 71.3 us (0.18)
  waiting for transfers between devices: 359 us -> 0 us
  Pallas kernels: 0 us -> 64.7 us
  between operations: 13.8 us -> 0.65 us
  matrix products: 11.7 us -> 0 us
  local copies, waits for them, and re-layouts: 11.7 us -> 5.79 us
    reduce_scatter x1 -> x0, waiting for transfers between devices: 209 us -> none  [body(): lax.psum_scatter(partial_sums, 'row', scatter_dimension=0, tiled=True)]
    all_gather x2 -> x0, waiting for transfers between devices: 149 us -> none  [the longest x1 75.5 us: body(): all_rows = lax.all_gather(activations, 'row', axis=0, tiled=True)]
    pallas_call x0 -> x1, Pallas kernels: none -> 64.7 us  [body(): pl.pallas_call(kernel, out_shape=(jax.ShapeDtypeStruct((hidden, width), B...]
    dot_general x2 -> x0, matrix products: 11.7 us -> none  [the longest x1 5.91 us: contract_rows(): lax.dot_general(left, right, (((0,), (0,)), ((), ())), preferred_element_...]
    gather x1 -> x0, local copies, waits for them, and re-layouts: 7.87 us -> none  [body(): aligned = jnp.take(gathered, row_order, axis=0)]
  transfers between devices with their start and end apart: 3 -> 0, of which waited for: 3 -> 0; matrix products, arithmetic and copies ran while one was open for 6% -> 0% of each run, Pallas kernels for 0% -> 0%
where the time goes in v1:
time: 71.3 us; the launch traced here: 71.1 us
  Pallas kernels  64.7 us (91%)
  local copies, waits for them, and re-layouts  5.79 us (8%)
    pallas_call x1, Pallas kernels, body(): pl.pallas_call(kernel, out_shape=(jax.ShapeDtypeStruct((hidden, width), B...  64.7 us
    unnamed x10, local copies, waits for them, and re-layouts  5.79 us

profile of v1, /device:TPU:1, one launch (start us, length us, event | category | flops | bytes accessed | tf_op | source)
XLA Modules:
  0.0 71.1 jit_solution(16840847000270727296)
XLA Ops:
  0.6 0.0 copy-start
  0.6 1.5 %copy-done = bf16[896,1024]{1,0:T(8,128)(2,1)S(1)} copy-done((bf16[896,1024]{1,0:T(8,128)(2,1)S(1)}, bf16[896,1024]{1,0:T(8,128)(2,1)}, u32[]{:S(2)}) %copy-start) | copy-done | bytes 1835032
  2.1 0.0 copy-start.1
  2.1 0.9 %copy-done.1 = bf16[64,896]{1,0:T(8,128)(2,1)S(1)} copy-done((bf16[64,896]{1,0:T(8,128)(2,1)S(1)}, bf16[64,896]{1,0:T(8,128)(2,1)}, u32[]{:S(2)}) %copy-start.1) | copy-done | bytes 114712
  3.0 0.0 copy-start.2
  3.0 0.8 %copy-done.2 = bf16[32,1024]{1,0:T(8,128)(2,1)S(1)} copy-done((bf16[32,1024]{1,0:T(8,128)(2,1)S(1)}, bf16[32,1024]{1,0:T(8,128)(2,1)}, u32[]{:S(2)}) %copy-start.2) | copy-done | bytes 65560
  3.9 0.0 copy-start.3
  3.9 0.7 copy-done.3
  4.6 64.7 %shard_map.59 = (bf16[896,1024]{1,0:T(8,128)(2,1)S(1)}, bf16[64,896]{1,0:T(8,128)(2,1)S(1)}) custom-call(bf16[64,896]{1,0:T(8,128)(2,1)S(1)} %copy-done.1, bf16[32,1024]{1,0:T(8,128)(2,1)S(1)} %copy-done.2, bf16[896,1024]{1,0:T(8,128)(2,1)S(1)} %copy-done, s32[8,128]{1,0:T(8,128)S(1)} %bitcast.1), custom_call_target="tpu_custom_call" | custom-call | tf_op jit(solution)/shard_map/pallas_call | solution.py:292
  69.2 1.2 %copy.8 = bf16[896,1024]{1,0:T(8,128)(2,1)} copy(bf16[896,1024]{1,0:T(8,128)(2,1)S(1)} %get-tuple-element.4) | data formatting | bytes 3670016
  70.5 0.6 copy.9
Async XLA Ops:
  0.6 1.5 %copy-start = (bf16[896,1024]{1,0:T(8,128)(2,1)S(1)}, bf16[896,1024]{1,0:T(8,128)(2,1)}, u32[]{:S(2)}) copy-start(bf16[896,1024]{1,0:T(8,128)(2,1)} %weight.1) | copy-start | bytes 5505028
  2.1 0.9 %copy-start.1 = (bf16[64,896]{1,0:T(8,128)(2,1)S(1)}, bf16[64,896]{1,0:T(8,128)(2,1)}, u32[]{:S(2)}) copy-start(bf16[64,896]{1,0:T(8,128)(2,1)} %act.1) | copy-start | bytes 344068
  3.0 0.8 %copy-start.2 = (bf16[32,1024]{1,0:T(8,128)(2,1)S(1)}, bf16[32,1024]{1,0:T(8,128)(2,1)}, u32[]{:S(2)}) copy-start(bf16[32,1024]{1,0:T(8,128)(2,1)} %cot.1) | copy-start | bytes 196612
  3.9 0.7 copy-start.3

commit v2 on v1

v2 whole, which is shorter than its diff:
```python
import jax
import jax.numpy as jnp
from jax import lax
from jax.experimental import pallas as pl
from jax.experimental.pallas import tpu as pltpu
from jax.sharding import PartitionSpec as P

MESH = pl.DeviceIdType.MESH
RING = 8
FAR = RING // 2
GROUPS = [(FAR, 0), (FAR, 1)]
for _d in (3, 2, 1):
    GROUPS += [(_d, 0), (_d, 1), (-_d, 0), (-_d, 1)]
GROUPS += [(0, 0), (0, 1)]
PLACE = {g: i for i, g in enumerate(GROUPS)}
DISTANCES = [4, 3, -3, 2, -2, 1, -1, 0]
SPLIT = 512
F32 = jnp.float32
BF16 = jnp.bfloat16
I16 = jnp.int16


def z_place(distance, half):
    return PLACE[(FAR if abs(distance) == FAR else distance, half)]


def hops(direction, stream):
    return FAR if (direction == 1) == (stream == 0) else FAR - 1


STREAMS = [(d, s) for s in (0, 1) for d in (1, -1)]


def dot_nt(a, b):
    return lax.dot_general(a, b, (((1,), (1,)), ((), ())), preferred_element_type=F32)


def dot_tn(a, b):
    return lax.dot_general(a, b, (((0,), (0,)), ((), ())), preferred_element_type=F32)


def kernel(
    act, cot, weight, order, wgrad, igrad,
    cot_all, act_all, w_vmem, order_vmem, place_col, pick, aligned, partial, wgrad_vmem, igrad_vmem,
    za_out, za_out_s, za_in, za_in_s, xb_out, xb_out_s, xb_in, xb_in_s, zb_out, zb_out_s, zb_in, zb_in_s,
    g_send, g_recv, s_send, s_recv, a_send, a_recv,
    za_sem, xb_sem, zb_sem, local_sem,
):
    row, col = lax.axis_index("row"), lax.axis_index("col")
    xh, z = row // RING, lax.rem(row, RING)
    y, xl, core = col // 4, lax.rem(col, 4) // 2, lax.rem(col, 2)

    def at_z(step):
        return (xh * RING + lax.rem(z + step + RING, RING), col)

    def at_y(step):
        return (row, lax.rem(y + step + RING, RING) * 4 + xl * 2 + core)

    x_far = ((1 - xh) * RING + z, col)
    x_near = (row, y * 4 + (1 - xl) * 2 + core)
    sibling = (row, y * 4 + xl * 2 + 1 - core)

    rows_g = cot.shape[0]
    rows_a, hidden = act.shape
    total = cot_all.shape[0]
    half = total // 2
    rows_h = rows_a // 2

    def g_slot(core_d, y_d, x_d):
        return cot_all.at[pl.ds(core_d * half + ((y_d % RING) * 2 + x_d) * rows_g, rows_g)]

    def g_half(ref, d):
        return ref.at[pl.ds(0 if d == 1 else rows_g // 2, rows_g // 2)]

    def a_rows(distance, h):
        return pl.ds(z_place(distance, h) * rows_a, rows_a)

    def remote(src, dst, send, recv, device):
        return pltpu.make_async_remote_copy(
            src_ref=src, dst_ref=dst, send_sem=send, recv_sem=recv, device_id=device, device_id_type=MESH
        )

    barrier = pltpu.get_barrier_semaphore()
    partners = (at_y(1), at_y(-1), at_y(2), at_y(-2), x_near, sibling, at_z(1), at_z(-1), x_far)
    for device in partners:
        pl.semaphore_signal(barrier, inc=1, device_id=device, device_id_type=MESH)

    own_order = pltpu.make_async_copy(order, order_vmem, local_sem.at[3])
    own_g = pltpu.make_async_copy(cot, g_slot(0, 0, 0), local_sem.at[0])
    own_a = pltpu.make_async_copy(act, act_all.at[a_rows(0, 0)], local_sem.at[1])
    own_w = pltpu.make_async_copy(weight, w_vmem, local_sem.at[2])
    own_order.start()
    own_g.start()
    own_a.start()
    own_w.start()
    pl.semaphore_wait(barrier, len(partners))

    sent = []

    def start(copy):
        copy.start()
        sent.append(copy)
        return copy

    g_count = [0]

    def g_copy(src, dst, device):
        n = g_count[0]
        g_count[0] += 1
        return remote(src, dst, g_send.at[n], g_recv.at[n], device)

    own2 = {d: g_copy(cot, g_slot(0, -2 * d, 0), at_y(2 * d)) for d in (1, -1)}
    own1 = {d: g_copy(cot, g_slot(0, -d, 0), at_y(d)) for d in (1, -1)}
    near0 = g_copy(cot, g_slot(0, 0, 1), x_near)
    near2 = {d: g_copy(g_slot(0, -2 * d, 0), g_slot(0, -2 * d, 1), x_near) for d in (1, -1)}
    far3 = {d: g_copy(g_slot(0, -2 * d, 0), g_slot(0, -3 * d, 0), at_y(d)) for d in (1, -1)}
    far4 = {d: g_copy(g_half(g_slot(0, -2 * d, 0), d), g_half(g_slot(0, FAR, 0), d), at_y(2 * d)) for d in (1, -1)}
    near4 = g_copy(g_slot(0, FAR, 0), g_slot(0, FAR, 1), x_near)
    side1 = {d: g_copy(g_slot(0, 0, 1), g_slot(0, -d, 1), at_y(d)) for d in (1, -1)}
    side3 = {d: g_copy(g_slot(0, -2 * d, 1), g_slot(0, -3 * d, 1), at_y(d)) for d in (1, -1)}
    shared = {}
    for y_d in range(RING):
        for x_d in range(2):
            i = y_d * 2 + x_d
            src = cot if i == 0 else g_slot(0, y_d, x_d)
            shared[(y_d, x_d)] = remote(src, g_slot(1, y_d, x_d), s_send.at[i], s_recv.at[i], sibling)

    def share(y_d, x_d):
        start(shared[(y_d % RING, x_d)])

    a_ring = {}
    n = 0
    for step in range(1, FAR + 1):
        for d, s in STREAMS:
            if step <= hops(d, s):
                src = act if (step == 1 and s == 0) else act_all.at[a_rows(-d * (step - 1), s)]
                a_ring[(step, d, s)] = remote(src, act_all.at[a_rows(-d * step, s)], a_send.at[n], a_recv.at[n], at_z(d))
                n += 1
    a_far = remote(act, act_all.at[a_rows(0, 1)], a_send.at[n], a_recv.at[n], x_far)

    def a_hop(step, s):
        for d in (1, -1):
            if step <= hops(d, s):
                a_ring[(step, d, s)].wait_recv()
                if step < hops(d, s):
                    start(a_ring[(step + 1, d, s)])

    start(own2[1])
    start(own2[-1])
    start(near0)
    start(own1[1])
    start(own1[-1])
    start(a_ring[(1, 1, 0)])
    start(a_ring[(1, -1, 0)])
    start(a_far)
    share(0, 0)

    own_order.wait()
    r = order_vmem[...]
    spot = (
        lax.rem(r // 32 + core, 2) * half
        + lax.rem(r // 128 - y + RING, RING) * (2 * rows_g)
        + lax.rem(r // 64 + xl, 2) * rows_g
        + lax.rem(r, 32)
    ).astype(F32)
    for b in range(total // 128):
        place_col[b * 128:(b + 1) * 128, :] = jnp.transpose(jnp.broadcast_to(spot[b:b + 1, :], (128, 128)))

    lanes = lax.broadcasted_iota(jnp.int32, (rows_a, 128), 1).astype(F32)

    def build_pick(first, last):
        for i in range(first, last):
            distance, h = GROUPS[i]
            shard = lax.rem(xh + h, 2) * RING + lax.rem(z + distance + RING, RING)
            want = place_col[pl.ds(pl.multiple_of(shard * rows_a, rows_a), rows_a), :]
            for j in range(total // 128):
                hit = jnp.where(want == lanes + float(j * 128), 1.0, 0.0).astype(F32)
                pick[i * rows_a:(i + 1) * rows_a, j * 128:(j + 1) * 128] = hit.astype(BF16)

    build_pick(0, 4)
    near0.wait_recv()
    start(side1[1])
    start(side1[-1])
    share(0, 1)
    build_pick(4, 8)
    for d in (1, -1):
        own2[d].wait_recv()
        start(far4[d])
        start(far3[d])
        start(near2[d])
        share(-2 * d, 0)
    a_far.wait_recv()
    start(a_ring[(1, 1, 1)])
    start(a_ring[(1, -1, 1)])
    a_hop(1, 0)
    for d in (1, -1):
        own1[d].wait_recv()
        share(-d, 0)
    build_pick(8, 12)
    for d in (1, -1):
        side1[d].wait_recv()
        share(-d, 1)
    for d in (1, -1):
        near2[d].wait_recv()
        start(side3[d])
        share(-2 * d, 1)
    far4[1].wait_recv()
    far4[-1].wait_recv()
    start(near4)
    share(FAR, 0)
    for d in (1, -1):
        far3[d].wait_recv()
        share(-3 * d, 0)
    build_pick(12, 16)
    a_hop(2, 0)
    a_hop(1, 1)
    for d in (1, -1):
        side3[d].wait_recv()
        share(-3 * d, 1)
    near4.wait_recv()
    share(FAR, 1)
    own_g.wait()
    own_w.wait()
    for key in shared:
        shared[key].wait_recv()

    def sums(first, last):
        rows = slice(first * rows_a, last * rows_a)
        aligned[rows, :] = jnp.dot(pick[rows, :], cot_all[...], preferred_element_type=F32).astype(BF16)
        partial[rows, :] = dot_nt(aligned[rows, :], w_vmem[...])

    def part_a(distance, h):
        i = z_place(distance, h)
        return partial[i * rows_a:(i + 1) * rows_a, :SPLIT]

    def part_b(distance, h):
        i = z_place(distance, h)
        return partial[i * rows_a:(i + 1) * rows_a, SPLIT:]

    def encode(value, out, scale):
        top = jnp.maximum(jnp.max(jnp.abs(value), axis=0, keepdims=True), 1e-34)
        out[...] = jnp.round(value * (32767.0 / top)).astype(jnp.int32).astype(I16)
        scale[...] = top * (1.0 / 32767.0)

    def decode(data, scale):
        return data[...].astype(jnp.int32).astype(F32) * scale[...]

    class Parcel:
        def __init__(self, refs, sems, slot, device, rows=None):
            out, out_s, got, got_s = (ref.at[slot] for ref in refs)
            if rows is not None:
                out, got = out.at[pl.ds(0, rows)], got.at[pl.ds(0, rows)]
            self.out, self.out_s, self.got, self.got_s = out, out_s, got, got_s
            self.data = remote(out, got, sems.at[0, slot], sems.at[1, slot], device)
            self.scale = remote(out_s, got_s, sems.at[2, slot], sems.at[3, slot], device)

        def post(self, value):
            encode(value, self.out, self.out_s)
            start(self.data)
            start(self.scale)

        def fetch(self):
            self.data.wait_recv()
            self.scale.wait_recv()
            return decode(self.got, self.got_s)

    za_refs = (za_out, za_out_s, za_in, za_in_s)
    za = {}
    for level in range(FAR, 0, -1):
        for d, h in STREAMS:
            if level <= hops(d, h):
                za[(level, d, h)] = Parcel(za_refs, za_sem, len(za), at_z(d))
    xa = Parcel(za_refs, za_sem, len(za), x_far)
    xb = {g: Parcel((xb_out, xb_out_s, xb_in, xb_in_s), xb_sem, i, x_far) for i, g in enumerate(DISTANCES)}
    zb = {}
    for level in range(FAR, 0, -1):
        for d in (1, -1):
            rows = rows_h if level == FAR else None
            zb[(level, d)] = Parcel((zb_out, zb_out_s, zb_in, zb_in_s), zb_sem, len(zb), at_z(d), rows)

    def a_first(level, d, h):
        za[(level, d, h)].post(part_a(level * d, h))

    def a_next(level, d, h):
        za[(level, d, h)].post(za[(level + 1, d, h)].fetch() + part_a(level * d, h))

    def b_cross(distance):
        xb[distance].post(part_b(distance, 1))

    def b_first():
        value = part_b(FAR, 0) + xb[FAR].fetch()
        zb[(FAR, 1)].post(value[:rows_h])
        zb[(FAR, -1)].post(value[rows_h:])

    def b_next(level, d):
        value = part_b(level * d, 0) + xb[level * d].fetch()
        got = zb[(level + 1, d)].fetch()
        if level + 1 < FAR:
            value = value + got
        elif d == 1:
            value = jnp.concatenate([value[:rows_h] + got, value[rows_h:]], axis=0)
        else:
            value = jnp.concatenate([value[:rows_h], value[rows_h:] + got], axis=0)
        zb[(level, d)].post(value)

    stored = []

    def wgrad_tiles(first, last):
        def tile(t, carry):
            at = pl.ds(pl.multiple_of(t * 128, 128), 128)
            wgrad_vmem[at, :] = dot_tn(act_all[:, at], aligned[...]).astype(BF16)
            return carry

        lax.fori_loop(first, last, tile, 0)
        rows = pl.ds(first * 128, (last - first) * 128)
        copy = pltpu.make_async_copy(wgrad_vmem.at[rows], wgrad.at[rows], local_sem.at[4 + len(stored)])
        copy.start()
        stored.append(copy)

    sums(0, 2)
    a_first(4, 1, 0)
    a_first(4, -1, 1)
    b_cross(4)
    sums(2, 6)
    a_first(3, 1, 1)
    a_first(3, -1, 0)
    b_cross(3)
    b_cross(-3)
    sums(6, 10)
    b_cross(2)
    b_cross(-2)
    a_next(3, 1, 0)
    a_next(3, -1, 1)
    b_first()
    a_hop(3, 0)
    sums(10, 14)
    b_cross(1)
    b_cross(-1)
    a_next(2, 1, 1)
    a_next(2, -1, 0)
    sums(14, 16)
    b_cross(0)
    b_next(3, 1)
    b_next(3, -1)
    a_next(2, 1, 0)
    a_next(2, -1, 1)
    a_hop(2, 1)
    a_next(1, 1, 1)
    a_next(1, -1, 0)
    a_hop(4, 0)
    b_next(2, 1)
    b_next(2, -1)
    a_next(1, 1, 0)
    a_next(1, -1, 1)
    a_hop(3, 1)
    b_next(1, 1)
    b_next(1, -1)
    a_hop(4, 1)
    own_a.wait()
    wgrad_tiles(0, 2)
    xa.post(part_a(0, 1) + za[(1, 1, 1)].fetch() + za[(1, -1, 1)].fetch())
    home_b = part_b(0, 0) + xb[0].fetch() + zb[(1, 1)].fetch() + zb[(1, -1)].fetch()
    igrad_vmem[:, SPLIT:] = home_b.astype(BF16)
    partial[:rows_a, :SPLIT] = part_a(0, 0) + za[(1, -1, 0)].fetch() + za[(1, 1, 0)].fetch()
    wgrad_tiles(2, 7)
    igrad_vmem[:, :SPLIT] = (partial[:rows_a, :SPLIT] + xa.fetch()).astype(BF16)
    copy = pltpu.make_async_copy(igrad_vmem, igrad, local_sem.at[4 + len(stored)])
    copy.start()
    stored.append(copy)
    for copy in sent:
        copy.wait_send()
    for copy in stored:
        copy.wait()


def body(activations, cotangent, down_weight, row_order):
    rows_a, hidden = activations.shape
    rows_g, width = cotangent.shape
    total = row_order.shape[0]
    hbm = pl.BlockSpec(memory_space=pltpu.HBM)
    dma = pltpu.SemaphoreType.DMA

    def parcels(slots, columns):
        return [
            pltpu.VMEM((slots, rows_a, columns), I16),
            pltpu.VMEM((slots, 1, columns), F32),
            pltpu.VMEM((slots, rows_a, columns), I16),
            pltpu.VMEM((slots, 1, columns), F32),
        ]

    return pl.pallas_call(
        kernel,
        out_shape=(
            jax.ShapeDtypeStruct((hidden, width), BF16),
            jax.ShapeDtypeStruct((rows_a, hidden), BF16),
        ),
        in_specs=[hbm] * 4,
        out_specs=(hbm, hbm),
        scratch_shapes=[
            pltpu.VMEM((total, width), BF16),
            pltpu.VMEM((total, hidden), BF16),
            pltpu.VMEM((hidden, width), BF16),
            pltpu.VMEM((total // 128, 128), jnp.int32),
            pltpu.VMEM((total, 128), F32),
            pltpu.VMEM((total, total), BF16),
            pltpu.VMEM((total, width), BF16),
            pltpu.VMEM((total, hidden), F32),
            pltpu.VMEM((hidden, width), BF16),
            pltpu.VMEM((rows_a, hidden), BF16),
            *parcels(15, SPLIT),
            *parcels(8, hidden - SPLIT),
            *parcels(8, hidden - SPLIT),
            dma((16,)), dma((16,)), dma((16,)), dma((16,)), dma((15,)), dma((15,)),
            dma((4, 15)), dma((4, 8)), dma((4, 8)), dma((8,)),
        ],
        compiler_params=pltpu.CompilerParams(
            collective_id=0, has_side_effects=True, vmem_limit_bytes=62 * 1024 * 1024
        ),
    )(activations, cotangent, down_weight, row_order.reshape(total // 128, 128))


def solution(mesh):
    in_specs = (P("row", "col"), P("col", "row"), P("col", "row"), P())
    out_specs = (P("col", "row"), P("row", "col"))
    return jax.shard_map(body, mesh=mesh, in_specs=in_specs, out_specs=out_specs, check_vma=False)
```

time: 71.3 us -> 63.7 us (0.89)
  Pallas kernels: 64.7 us -> 59.3 us
  local copies, waits for them, and re-layouts: 5.79 us -> 3.56 us
    pallas_call x1, Pallas kernels: 64.7 us -> 59.3 us  [body(): pl.pallas_call(kernel, out_shape=(jax.ShapeDtypeStruct((hidden, width), B...]
    unnamed x10 -> x4, local copies, waits for them, and re-layouts: 5.79 us -> 3.56 us
where the time goes in v2:
time: 63.7 us; the launch traced here: 63.5 us
  Pallas kernels  59.3 us (93%)
  local copies, waits for them, and re-layouts  3.56 us (6%)
  between operations  0.65 us (1%)
    pallas_call x1, Pallas kernels, body(): pl.pallas_call(kernel, out_shape=(jax.ShapeDtypeStruct((hidden, width), B...  59.3 us
    unnamed x4, local copies, waits for them, and re-layouts  3.56 us

profile of v2, /device:TPU:1, one launch (start us, length us, event | category | flops | bytes accessed | tf_op | source)
XLA Modules:
  0.0 63.5 jit_solution(2679600640227755367)
XLA Ops:
  0.6 59.3 %shard_map.59 = (bf16[896,1024]{1,0:T(8,128)(2,1)}, bf16[64,896]{1,0:T(8,128)(2,1)}) custom-call(bf16[64,896]{1,0:T(8,128)(2,1)} %act.1, bf16[32,1024]{1,0:T(8,128)(2,1)} %cot.1, bf16[896,1024]{1,0:T(8,128)(2,1)} %weight.1, s32[8,128]{1,0:T(8,128)} %bitcast.1), custom_call_target="tpu_custom_call" | custom-call | tf_op jit(solution)/shard_map/pallas_call | solution.py:391
  60.0 0.0 copy-start
  60.0 2.9 %copy.8 = bf16[896,1024]{1,0:T(8,128)(2,1)} copy(bf16[896,1024]{1,0:T(8,128)(2,1)} %get-tuple-element.4) | data formatting | bytes 3670016
  62.9 0.0 copy-done
  62.9 0.6 %copy.9 = bf16[64,896]{1,0:T(8,128)(2,1)} copy(bf16[64,896]{1,0:T(8,128)(2,1)S(1)} %copy-done) | data formatting | bytes 229376
Async XLA Ops:
  60.0 2.9 %copy-start = (bf16[64,896]{1,0:T(8,128)(2,1)S(1)}, bf16[64,896]{1,0:T(8,128)(2,1)}, u32[]{:S(2)}) copy-start(bf16[64,896]{1,0:T(8,128)(2,1)} %get-tuple-element.5) | copy-start | bytes 344068

commit v3 on v2

--- a/solution.py
+++ b/solution.py
@@ -41,7 +41,7 @@
 
 def kernel(
     act, cot, weight, order, wgrad, igrad,
-    cot_all, act_all, w_vmem, order_vmem, place_col, pick, aligned, partial, wgrad_vmem, igrad_vmem,
+    cot_all, act_all, w_vmem, order_vmem, place_col, pick, aligned, partial,
     za_out, za_out_s, za_in, za_in_s, xb_out, xb_out_s, xb_in, xb_in_s, zb_out, zb_out_s, zb_in, zb_in_s,
     g_send, g_recv, s_send, s_recv, a_send, a_recv,
     za_sem, xb_sem, zb_sem, local_sem,
@@ -81,7 +81,7 @@
         )
 
     barrier = pltpu.get_barrier_semaphore()
-    partners = (at_y(1), at_y(-1), at_y(2), at_y(-2), x_near, sibling, at_z(1), at_z(-1), x_far)
+    partners = (at_y(1), at_y(-1), at_y(2), at_y(-2), x_near, sibling, at_z(1), at_z(-1), at_z(2), at_z(-2), x_far)
     for device in partners:
         pl.semaphore_signal(barrier, inc=1, device_id=device, device_id_type=MESH)
 
@@ -115,9 +115,9 @@
     near2 = {d: g_copy(g_slot(0, -2 * d, 0), g_slot(0, -2 * d, 1), x_near) for d in (1, -1)}
     far3 = {d: g_copy(g_slot(0, -2 * d, 0), g_slot(0, -3 * d, 0), at_y(d)) for d in (1, -1)}
     far4 = {d: g_copy(g_half(g_slot(0, -2 * d, 0), d), g_half(g_slot(0, FAR, 0), d), at_y(2 * d)) for d in (1, -1)}
-    near4 = g_copy(g_slot(0, FAR, 0), g_slot(0, FAR, 1), x_near)
     side1 = {d: g_copy(g_slot(0, 0, 1), g_slot(0, -d, 1), at_y(d)) for d in (1, -1)}
     side3 = {d: g_copy(g_slot(0, -2 * d, 1), g_slot(0, -3 * d, 1), at_y(d)) for d in (1, -1)}
+    side4 = {d: g_copy(g_half(g_slot(0, -2 * d, 1), d), g_half(g_slot(0, FAR, 1), d), at_y(2 * d)) for d in (1, -1)}
     shared = {}
     for y_d in range(RING):
         for x_d in range(2):
@@ -189,10 +189,10 @@
         start(far3[d])
         start(near2[d])
         share(-2 * d, 0)
+    a_hop(1, 0)
     a_far.wait_recv()
     start(a_ring[(1, 1, 1)])
     start(a_ring[(1, -1, 1)])
-    a_hop(1, 0)
     for d in (1, -1):
         own1[d].wait_recv()
         share(-d, 0)
@@ -202,23 +202,25 @@
         share(-d, 1)
     for d in (1, -1):
         near2[d].wait_recv()
+        start(side4[d])
         start(side3[d])
         share(-2 * d, 1)
+    a_hop(2, 0)
     far4[1].wait_recv()
     far4[-1].wait_recv()
-    start(near4)
     share(FAR, 0)
     for d in (1, -1):
         far3[d].wait_recv()
         share(-3 * d, 0)
     build_pick(12, 16)
-    a_hop(2, 0)
     a_hop(1, 1)
     for d in (1, -1):
         side3[d].wait_recv()
         share(-3 * d, 1)
-    near4.wait_recv()
+    side4[1].wait_recv()
+    side4[-1].wait_recv()
     share(FAR, 1)
+    a_hop(3, 0)
     own_g.wait()
     own_w.wait()
     for key in shared:
@@ -303,74 +305,62 @@
             value = jnp.concatenate([value[:rows_h], value[rows_h:] + got], axis=0)
         zb[(level, d)].post(value)
 
-    stored = []
-
     def wgrad_tiles(first, last):
         def tile(t, carry):
             at = pl.ds(pl.multiple_of(t * 128, 128), 128)
-            wgrad_vmem[at, :] = dot_tn(act_all[:, at], aligned[...]).astype(BF16)
+            wgrad[at, :] = dot_tn(act_all[:, at], aligned[...]).astype(BF16)
             return carry
 
         lax.fori_loop(first, last, tile, 0)
-        rows = pl.ds(first * 128, (last - first) * 128)
-        copy = pltpu.make_async_copy(wgrad_vmem.at[rows], wgrad.at[rows], local_sem.at[4 + len(stored)])
-        copy.start()
-        stored.append(copy)
 
     sums(0, 2)
+    a_first(4, -1, 1)
     a_first(4, 1, 0)
-    a_first(4, -1, 1)
     b_cross(4)
     sums(2, 6)
     a_first(3, 1, 1)
     a_first(3, -1, 0)
     b_cross(3)
     b_cross(-3)
+    a_hop(2, 1)
+    a_next(3, -1, 1)
+    a_next(3, 1, 0)
     sums(6, 10)
+    b_first()
     b_cross(2)
     b_cross(-2)
-    a_next(3, 1, 0)
-    a_next(3, -1, 1)
-    b_first()
-    a_hop(3, 0)
-    sums(10, 14)
+    a_next(2, 1, 1)
+    a_next(2, -1, 0)
+    sums(10, 16)
+    b_next(3, 1)
+    b_next(3, -1)
     b_cross(1)
     b_cross(-1)
-    a_next(2, 1, 1)
-    a_next(2, -1, 0)
-    sums(14, 16)
-    b_cross(0)
-    b_next(3, 1)
-    b_next(3, -1)
+    a_next(2, -1, 1)
     a_next(2, 1, 0)
-    a_next(2, -1, 1)
-    a_hop(2, 1)
+    a_hop(3, 1)
     a_next(1, 1, 1)
     a_next(1, -1, 0)
-    a_hop(4, 0)
     b_next(2, 1)
     b_next(2, -1)
+    b_cross(0)
+    a_next(1, -1, 1)
     a_next(1, 1, 0)
-    a_next(1, -1, 1)
-    a_hop(3, 1)
+    a_hop(4, 0)
+    a_hop(4, 1)
+    own_a.wait()
     b_next(1, 1)
     b_next(1, -1)
-    a_hop(4, 1)
-    own_a.wait()
     wgrad_tiles(0, 2)
     xa.post(part_a(0, 1) + za[(1, 1, 1)].fetch() + za[(1, -1, 1)].fetch())
+    wgrad_tiles(2, 5)
+    partial[:rows_a, :SPLIT] = part_a(0, 0) + za[(1, -1, 0)].fetch() + za[(1, 1, 0)].fetch()
     home_b = part_b(0, 0) + xb[0].fetch() + zb[(1, 1)].fetch() + zb[(1, -1)].fetch()
-    igrad_vmem[:, SPLIT:] = home_b.astype(BF16)
-    partial[:rows_a, :SPLIT] = part_a(0, 0) + za[(1, -1, 0)].fetch() + za[(1, 1, 0)].fetch()
-    wgrad_tiles(2, 7)
-    igrad_vmem[:, :SPLIT] = (partial[:rows_a, :SPLIT] + xa.fetch()).astype(BF16)
-    copy = pltpu.make_async_copy(igrad_vmem, igrad, local_sem.at[4 + len(stored)])
-    copy.start()
-    stored.append(copy)
+    igrad[:, SPLIT:] = home_b.astype(BF16)
+    wgrad_tiles(5, 7)
+    igrad[:, :SPLIT] = (partial[:rows_a, :SPLIT] + xa.fetch()).astype(BF16)
     for copy in sent:
         copy.wait_send()
-    for copy in stored:
-        copy.wait()
 
 
 def body(activations, cotangent, down_weight, row_order):
@@ -388,6 +378,7 @@
             pltpu.VMEM((slots, 1, columns), F32),
         ]
 
+    operands = (activations, cotangent, down_weight, row_order.reshape(total // 128, 128))
     return pl.pallas_call(
         kernel,
         out_shape=(
@@ -395,7 +386,7 @@
             jax.ShapeDtypeStruct((rows_a, hidden), BF16),
         ),
         in_specs=[hbm] * 4,
-        out_specs=(hbm, hbm),
+        out_specs=(pl.BlockSpec(memory_space=pltpu.VMEM),) * 2,
         scratch_shapes=[
             pltpu.VMEM((total, width), BF16),
             pltpu.VMEM((total, hidden), BF16),
@@ -405,18 +396,16 @@
             pltpu.VMEM((total, total), BF16),
             pltpu.VMEM((total, width), BF16),
             pltpu.VMEM((total, hidden), F32),
-            pltpu.VMEM((hidden, width), BF16),
-            pltpu.VMEM((rows_a, hidden), BF16),
             *parcels(15, SPLIT),
             *parcels(8, hidden - SPLIT),
             *parcels(8, hidden - SPLIT),
-            dma((16,)), dma((16,)), dma((16,)), dma((16,)), dma((15,)), dma((15,)),
-            dma((4, 15)), dma((4, 8)), dma((4, 8)), dma((8,)),
+            dma((17,)), dma((17,)), dma((16,)), dma((16,)), dma((15,)), dma((15,)),
+            dma((4, 15)), dma((4, 8)), dma((4, 8)), dma((4,)),
         ],
         compiler_params=pltpu.CompilerParams(
-            collective_id=0, has_side_effects=True, vmem_limit_bytes=62 * 1024 * 1024
+            collective_id=0, has_side_effects=True, vmem_limit_bytes=40 * 1024 * 1024
         ),
-    )(activations, cotangent, down_weight, row_order.reshape(total // 128, 128))
+    )(*(pltpu.with_memory_space_constraint(x, pltpu.HBM) for x in operands))
 
 
 def solution(mesh):

time: 63.7 us -> 59.2 us (0.929)
  the two profiles are of different devices: /device:TPU:1 before, /device:TPU:8 now
where the time goes in v3:
time: 59.2 us; the launch traced here: 59.1 us
  Pallas kernels  56.6 us (96%)
  local copies, waits for them, and re-layouts  1.88 us (3%)
  between operations  0.64 us (1%)
    pallas_call x1, Pallas kernels, body(): pl.pallas_call(kernel, out_shape=(jax.ShapeDtypeStruct((hidden, width), B...  56.6 us
    unnamed x2, local copies, waits for them, and re-layouts  1.88 us

profile of v3, /device:TPU:8, one launch (start us, length us, event | category | flops | bytes accessed | tf_op | source)
XLA Modules:
  0.0 59.1 jit_solution(14160673899372662215)
XLA Ops:
  0.6 56.6 %shard_map.59 = (bf16[896,1024]{1,0:T(8,128)(2,1)S(1)}, bf16[64,896]{1,0:T(8,128)(2,1)S(1)}) custom-call(bf16[64,896]{1,0:T(8,128)(2,1)} %act.1, bf16[32,1024]{1,0:T(8,128)(2,1)} %cot.1, bf16[896,1024]{1,0:T(8,128)(2,1)} %weight.1, s32[8,128]{1,0:T(8,128)} %bitcast.1), custom_call_target="tpu_custom_call" | custom-call | tf_op jit(solution)/shard_map/pallas_call | solution.py:382
  57.2 1.2 %copy.8 = bf16[896,1024]{1,0:T(8,128)(2,1)} copy(bf16[896,1024]{1,0:T(8,128)(2,1)S(1)} %get-tuple-element.4) | data formatting | bytes 3670016
  58.5 0.6 %copy.9 = bf16[64,896]{1,0:T(8,128)(2,1)} copy(bf16[64,896]{1,0:T(8,128)(2,1)S(1)} %get-tuple-element.5) | data formatting | bytes 229376

commit v4 on v3

--- a/solution.py
+++ b/solution.py
@@ -14,7 +14,7 @@
 GROUPS += [(0, 0), (0, 1)]
 PLACE = {g: i for i, g in enumerate(GROUPS)}
 DISTANCES = [4, 3, -3, 2, -2, 1, -1, 0]
-SPLIT = 512
+SPLIT = 256
 F32 = jnp.float32
 BF16 = jnp.bfloat16
 I16 = jnp.int16
@@ -278,7 +278,7 @@
     for level in range(FAR, 0, -1):
         for d in (1, -1):
             rows = rows_h if level == FAR else None
-            zb[(level, d)] = Parcel((zb_out, zb_out_s, zb_in, zb_in_s), zb_sem, len(zb), at_z(d), rows)
+            zb[(level, d)] = Parcel((zb_out, zb_out_s, zb_in, zb_in_s), zb_sem, len(zb), at_z(2 * d if level == FAR else d), rows)
 
     def a_first(level, d, h):
         za[(level, d, h)].post(part_a(level * d, h))
@@ -296,13 +296,14 @@
 
     def b_next(level, d):
         value = part_b(level * d, 0) + xb[level * d].fetch()
-        got = zb[(level + 1, d)].fetch()
-        if level + 1 < FAR:
-            value = value + got
-        elif d == 1:
-            value = jnp.concatenate([value[:rows_h] + got, value[rows_h:]], axis=0)
-        else:
-            value = jnp.concatenate([value[:rows_h], value[rows_h:] + got], axis=0)
+        if level < 3:
+            value = value + zb[(level + 1, d)].fetch()
+        if level == 2:
+            got = zb[(FAR, d)].fetch()
+            if d == 1:
+                value = jnp.concatenate([value[:rows_h] + got, value[rows_h:]], axis=0)
+            else:
+                value = jnp.concatenate([value[:rows_h], value[rows_h:] + got], axis=0)
         zb[(level, d)].post(value)
 
     def wgrad_tiles(first, last):
@@ -314,51 +315,49 @@
         lax.fori_loop(first, last, tile, 0)
 
     sums(0, 2)
+    b_cross(4)
     a_first(4, -1, 1)
     a_first(4, 1, 0)
-    b_cross(4)
     sums(2, 6)
+    b_cross(3)
+    b_cross(-3)
     a_first(3, 1, 1)
     a_first(3, -1, 0)
-    b_cross(3)
-    b_cross(-3)
     a_hop(2, 1)
+    sums(6, 10)
+    b_cross(2)
+    b_cross(-2)
+    b_first()
     a_next(3, -1, 1)
     a_next(3, 1, 0)
-    sums(6, 10)
-    b_first()
-    b_cross(2)
-    b_cross(-2)
-    a_next(2, 1, 1)
-    a_next(2, -1, 0)
     sums(10, 16)
     b_next(3, 1)
     b_next(3, -1)
     b_cross(1)
     b_cross(-1)
+    a_next(2, 1, 1)
+    a_next(2, -1, 0)
     a_next(2, -1, 1)
     a_next(2, 1, 0)
     a_hop(3, 1)
-    a_next(1, 1, 1)
-    a_next(1, -1, 0)
     b_next(2, 1)
     b_next(2, -1)
     b_cross(0)
+    a_next(1, 1, 1)
+    a_next(1, -1, 0)
     a_next(1, -1, 1)
     a_next(1, 1, 0)
+    b_next(1, 1)
+    b_next(1, -1)
     a_hop(4, 0)
     a_hop(4, 1)
     own_a.wait()
-    b_next(1, 1)
-    b_next(1, -1)
-    wgrad_tiles(0, 2)
     xa.post(part_a(0, 1) + za[(1, 1, 1)].fetch() + za[(1, -1, 1)].fetch())
-    wgrad_tiles(2, 5)
-    partial[:rows_a, :SPLIT] = part_a(0, 0) + za[(1, -1, 0)].fetch() + za[(1, 1, 0)].fetch()
+    wgrad_tiles(0, 7)
+    home_a = part_a(0, 0) + za[(1, -1, 0)].fetch() + za[(1, 1, 0)].fetch() + xa.fetch()
+    igrad[:, :SPLIT] = home_a.astype(BF16)
     home_b = part_b(0, 0) + xb[0].fetch() + zb[(1, 1)].fetch() + zb[(1, -1)].fetch()
     igrad[:, SPLIT:] = home_b.astype(BF16)
-    wgrad_tiles(5, 7)
-    igrad[:, :SPLIT] = (partial[:rows_a, :SPLIT] + xa.fetch()).astype(BF16)
     for copy in sent:
         copy.wait_send()
 

time: 59.2 us -> 57.2 us (0.966)
  the two profiles are of different devices: /device:TPU:8 before, /device:TPU:1 now
where the time goes in v4:
time: 57.2 us; the launch traced here: 56.7 us
  Pallas kernels  54.2 us (95%)
  local copies, waits for them, and re-layouts  1.88 us (3%)
  between operations  0.64 us (1%)
    pallas_call x1, Pallas kernels, body(): pl.pallas_call(kernel, out_shape=(jax.ShapeDtypeStruct((hidden, width), B...  54.2 us
    unnamed x2, local copies, waits for them, and re-layouts  1.88 us

profile of v4, /device:TPU:1, one launch (start us, length us, event | category | flops | bytes accessed | tf_op | source)
XLA Modules:
  0.0 56.7 jit_solution(14120440828757403267)
XLA Ops:
  0.6 54.2 %shard_map.59 = (bf16[896,1024]{1,0:T(8,128)(2,1)S(1)}, bf16[64,896]{1,0:T(8,128)(2,1)S(1)}) custom-call(bf16[64,896]{1,0:T(8,128)(2,1)} %act.1, bf16[32,1024]{1,0:T(8,128)(2,1)} %cot.1, bf16[896,1024]{1,0:T(8,128)(2,1)} %weight.1, s32[8,128]{1,0:T(8,128)} %bitcast.1), custom_call_target="tpu_custom_call" | custom-call | tf_op jit(solution)/shard_map/pallas_call | solution.py:381
  54.8 1.2 %copy.8 = bf16[896,1024]{1,0:T(8,128)(2,1)} copy(bf16[896,1024]{1,0:T(8,128)(2,1)S(1)} %get-tuple-element.4) | data formatting | bytes 3670016
  56.0 0.6 %copy.9 = bf16[64,896]{1,0:T(8,128)(2,1)} copy(bf16[64,896]{1,0:T(8,128)(2,1)S(1)} %get-tuple-element.5) | data formatting | bytes 229376

commit v5 on v4

--- a/solution.py
+++ b/solution.py
@@ -185,9 +185,9 @@
     build_pick(4, 8)
     for d in (1, -1):
         own2[d].wait_recv()
+        start(near2[d])
         start(far4[d])
         start(far3[d])
-        start(near2[d])
         share(-2 * d, 0)
     a_hop(1, 0)
     a_far.wait_recv()

time: 57.2 us -> 57.2 us (level)
  no operation moved by 1% of the time
where the time goes in v5:
time: 57.2 us; the launch traced here: 56.7 us
  Pallas kernels  54.2 us (95%)
  local copies, waits for them, and re-layouts  1.88 us (3%)
  between operations  0.64 us (1%)
    pallas_call x1, Pallas kernels, body(): pl.pallas_call(kernel, out_shape=(jax.ShapeDtypeStruct((hidden, width), B...  54.2 us
    unnamed x2, local copies, waits for them, and re-layouts  1.88 us

profile of v5, /device:TPU:1, one launch (start us, length us, event | category | flops | bytes accessed | tf_op | source)
XLA Modules:
  0.0 56.7 jit_solution(6111686866872099633)
XLA Ops:
  0.6 54.2 %shard_map.59 = (bf16[896,1024]{1,0:T(8,128)(2,1)S(1)}, bf16[64,896]{1,0:T(8,128)(2,1)S(1)}) custom-call(bf16[64,896]{1,0:T(8,128)(2,1)} %act.1, bf16[32,1024]{1,0:T(8,128)(2,1)} %cot.1, bf16[896,1024]{1,0:T(8,128)(2,1)} %weight.1, s32[8,128]{1,0:T(8,128)} %bitcast.1), custom_call_target="tpu_custom_call" | custom-call | tf_op jit(solution)/shard_map/pallas_call | solution.py:381
  54.8 1.2 %copy.8 = bf16[896,1024]{1,0:T(8,128)(2,1)} copy(bf16[896,1024]{1,0:T(8,128)(2,1)S(1)} %get-tuple-element.4) | data formatting | bytes 3670016
  56.0 0.6 %copy.9 = bf16[64,896]{1,0:T(8,128)(2,1)} copy(bf16[64,896]{1,0:T(8,128)(2,1)S(1)} %get-tuple-element.5) | data formatting | bytes 229376
